TPU v7x, 32 devices: a whole 2x2x4 slice. The times are simulated.
32 devices in a mesh: runs: 2 (over y), tile: 4 (over z), layer: 2 (over x), star: 2 (over core).
Axes of the slice: x: 2, y: 2, z: 4, core: 2. Of those that a mesh axis runs over, the one named last changes fastest.
Arguments:
- screens: float32 [12, 384, 1536], P(('runs', 'layer'), 'tile'), parts along dimension 0, may hold values from -6 to 6
- layer_weight: float32 [12], P(('runs', 'layer')), parts along dimension 0, may hold values from 0.3 to 1
- wind_row: int32 [12], P('runs'), parts along dimension 0, may hold values from -4 to 4, as said below
- wind_col: int32 [12], P('runs'), parts along dimension 0, may hold values from -4 to 4, as said below
- foot_row: int32 [6, 6], replicated, may hold values from -80 to 79, as said below
- foot_col: int32 [6, 6], replicated, may hold values from -80 to 79, as said below
- frac_row: float32 [6, 6], replicated, may hold values from 0 to 1
- frac_col: float32 [6, 6], replicated, may hold values from 0 to 1
- amplitude: float32 [384, 1536], P('tile', 'layer'), may hold values from 0.5 to 2
- valid: int32 [24, 96], P('tile', 'layer'), may hold values 0 or 1
- recon_matrix: bfloat16 [6, 2, 24, 96, 2688], P('star', None, 'tile', 'layer'), may hold values from -0.0390625 to 0.0390625
- prev_recon: float32 [5376], P('runs'), parts along dimension 0, may hold values from -6 to 6
Outputs:
- shifted: float32 [12, 384, 1536], P(('runs', 'layer'), 'tile'), parts along dimension 0
- slopes: float32 [12, 2, 24, 96], P(('runs', 'star'), None, 'tile', 'layer'), parts along dimension 0
- commands: float32 [5376], P('runs'), parts along dimension 0
There are 2 independent parts, one for each index of `runs`. A program takes and returns all parts, laid end to end along the dimension named above; an argument that names none is the same for every part. Nothing has to cross between parts.
Inputs may be any that keep to these rules, and one draw needn't show every extreme that they name: `wind_row`: some layer takes 4 and another takes -4. `wind_col`: some layer takes 4 and another takes -4. `foot_row`: some star and layer take -80 and another takes 80 - 1. `foot_col`: some star and layer take -80 and another takes 80 - 1.
All inputs are finite; a program needn't handle non-finite values. No bound on the sum of `valid` on one device may be relied on, other than what follows from the above.
Results may differ from a plain program's by a relative error of at most 0.0019.
Values sent between devices are 32-bit elements; how exact they have to be, the bound alone decides.
A program may use at most 64 MiB of HBM per device.

v0:
```python
import math
import jax
import jax.numpy as jnp
from jax import lax
from jax.sharding import PartitionSpec as P

PIX = 16
PAD = 32
WIND = 4
FOOT = 80


def with_halo(value, sides, width):
    for axis, dim in sides:
        size, length = (lax.axis_size(axis), value.shape[dim])
        up = [(i, (i + 1) % size) for i in range(size)]
        down = [(j, i) for i, j in up]
        last = lax.slice_in_dim(value, length - width, length, axis=dim)
        first = lax.slice_in_dim(value, 0, width, axis=dim)
        before = lax.ppermute(last, axis, up)
        after = lax.ppermute(first, axis, down)
        value = jnp.concatenate([before, value, after], axis=dim)
    return value


def roll_columns(values, amount):
    extent = values.shape[-1]
    begin = jnp.mod(-amount, extent)
    doubled = jnp.concatenate([values, values], axis=-1)
    return lax.dynamic_slice_in_dim(doubled, begin, extent, values.ndim - 1)


def sh_slopes(share, amplitude, valid):
    star_count, band_rows, band_cols = share.shape
    sub_rows = band_rows // PIX
    sub_cols = band_cols // PIX
    group = math.gcd(sub_cols, max(1, 128 // PIX))
    blocks = sub_cols // group
    freq_index = jnp.arange(PAD, dtype=jnp.int32)[:, None]
    pixel_index = jnp.arange(PIX, dtype=jnp.int32)[None, :]
    phases = 2.0 * math.pi / PAD * jnp.mod(freq_index * pixel_index, PAD).astype(jnp.float32)
    cosine = jnp.cos(phases)
    sine = jnp.sin(phases)
    identity = jnp.eye(group, dtype=jnp.float32)
    diag_cos = jnp.einsum("gh,vq->gqhv", identity, cosine).reshape(group * PIX, group * PAD)
    diag_sin = jnp.einsum("gh,vq->gqhv", identity, sine).reshape(group * PIX, group * PAD)
    table = jnp.concatenate(
        [
            jnp.concatenate([diag_cos, -diag_sin], axis=1),
            jnp.concatenate([diag_sin, diag_cos], axis=1),
        ],
        axis=0,
    )
    field_real = (amplitude * jnp.cos(share)).reshape(
        star_count, sub_rows, PIX, blocks, group * PIX
    )
    field_imag = (amplitude * jnp.sin(share)).reshape(
        star_count, sub_rows, PIX, blocks, group * PIX
    )
    stacked = jnp.concatenate([field_real, field_imag], axis=-1)
    highest = lax.Precision.HIGHEST
    half = jnp.einsum("sapnk,kj->sapnj", stacked, table, precision=highest)
    row_cos = jnp.einsum("sapnj,up->saunj", half, cosine, precision=highest)
    row_sin = jnp.einsum("sapnj,up->saunj", half, sine, precision=highest)
    width = group * PAD
    spec_real = row_cos[..., :width] + row_sin[..., width:]
    spec_imag = row_cos[..., width:] - row_sin[..., :width]
    intensity = (spec_real * spec_real + spec_imag * spec_imag).reshape(
        star_count, sub_rows, PAD, blocks, group, PAD
    )
    centred = (jnp.mod(jnp.arange(PAD, dtype=jnp.int32) + PAD // 2, PAD) - PAD // 2).astype(
        jnp.float32
    )
    summed = jnp.sum(intensity, axis=(2, 5))
    along_rows = jnp.sum(intensity * centred[None, None, :, None, None, None], axis=(2, 5)) / summed
    along_cols = jnp.sum(intensity * centred[None, None, None, None, None, :], axis=(2, 5)) / summed
    along_rows = along_rows.reshape(star_count, sub_rows, sub_cols)
    along_cols = along_cols.reshape(star_count, sub_rows, sub_cols)
    return jnp.stack([along_rows, along_cols], axis=1) * valid.astype(jnp.float32)


def body(
    screens,
    layer_weight,
    wind_row,
    wind_col,
    foot_row,
    foot_col,
    frac_row,
    frac_col,
    amplitude,
    valid,
    recon_matrix,
    prev_recon,
):
    lay_local, band_rows, extent = screens.shape
    star_local = recon_matrix.shape[0]
    layer_start = lax.axis_index("layer") * lay_local
    star_start = lax.axis_index("star") * star_local
    padded = with_halo(screens, (("tile", 1),), WIND)
    moved = []
    for j in range(lay_local):
        rolled = roll_columns(padded[j], wind_col[layer_start + j])
        moved.append(
            lax.dynamic_slice_in_dim(rolled, WIND - wind_row[layer_start + j], band_rows, 0)
        )
    shifted = jnp.stack(moved)
    source = with_halo(shifted, (("tile", 1),), FOOT)
    pupils = []
    for g in range(star_local):
        star_id = star_start + g
        pupil = jnp.zeros((band_rows, extent), jnp.float32)
        for j in range(lay_local):
            layer_id = layer_start + j
            row_frac = frac_row[star_id, layer_id]
            col_frac = frac_col[star_id, layer_id]
            rows_cut = lax.dynamic_slice_in_dim(
                source[j], FOOT + foot_row[star_id, layer_id], band_rows + 1, 0
            )
            doubled = jnp.concatenate([rows_cut, rows_cut], axis=1)
            window = lax.dynamic_slice_in_dim(
                doubled, jnp.mod(foot_col[star_id, layer_id], extent), extent + 1, 1
            )
            anchor = window[:-1, :-1]
            beside = window[:-1, 1:]
            lower = window[1:, :-1]
            corner = window[1:, 1:]
            sampled = (
                (1.0 - row_frac) * (1.0 - col_frac) * anchor
                + row_frac * (1.0 - col_frac) * lower
                + (1.0 - row_frac) * col_frac * beside
                + row_frac * col_frac * corner
            )
            pupil = pupil + layer_weight[j] * sampled
        pupils.append(pupil)
    partial_value = jnp.stack(pupils)
    block_cols = extent // lax.axis_size("layer")
    summed = lax.psum(partial_value, "layer")
    share = lax.dynamic_slice_in_dim(summed, lax.axis_index("layer") * block_cols, block_cols, 2)
    slopes = sh_slopes(share, amplitude, valid)
    local_terms = jnp.dot(
        slopes.astype(jnp.bfloat16).reshape(1, -1),
        recon_matrix.reshape(-1, recon_matrix.shape[-1]),
        preferred_element_type=jnp.float32,
    )[0]
    recon = lax.psum(local_terms, ("tile", "layer", "star"))
    commands = 2.0 * recon - prev_recon
    return (shifted, slopes, commands)


def solution(mesh):
    return jax.shard_map(
        body,
        mesh=mesh,
        in_specs=(
            P(("runs", "layer"), "tile", None),
            P(("runs", "layer")),
            P("runs"),
            P("runs"),
            P(),
            P(),
            P(),
            P(),
            P("tile", "layer"),
            P("tile", "layer"),
            P("star", None, "tile", "layer", None),
            P("runs"),
        ),
        out_specs=(
            P(("runs", "layer"), "tile", None),
            P(("runs", "star"), None, "tile", "layer"),
            P("runs"),
        ),
        check_vma=False,
    )
```

profile of v0, /device:TPU:0, one launch (start us, length us, event | category | flops | bytes accessed | tf_op | source)
XLA Modules:
  0.0 263.3 jit_solution(9699940544491723572)
XLA Ops:
  7.2 1.0 fusion.100
  8.2 3.1 %collective-permute-start = (f32[3,4,1536]{2,1,0:T(4,128)S(1)}, f32[3,4,1536]{2,1,0:T(4,128)S(1)}, u32[]{:S(2)}, u32[]{:S(2)}) collective-permute-start(f32[3,4,1536]{2,1,0:T(4,128)S(1)} %get-tuple-element.24), channel_id=1, source_target_pairs={{0,4},{4,8},{8,12},{12,0},{1,5},{5,9},{9,13},{13,1},{2,6},{6,10},{... | collective-permute-start | bytes 221192 | tf_op jit(solution)/shard_map/ppermute | solution.py:20
  11.3 2.1 collective-permute-start.1
  13.4 1.5 fusion.107
  20.8 1.7 pad_maximum_fusion.1
  24.0 2.1 fusion.99
  26.1 3.8 %collective-permute-start.3 = (f32[3,80,1536]{2,1,0:T(8,128)}, f32[3,80,1536]{2,1,0:T(8,128)}, u32[]{:S(2)}, u32[]{:S(2)}) collective-permute-start(f32[3,80,1536]{2,1,0:T(8,128)} %get-tuple-element.23), channel_id=1, source_target_pairs={{4,0},{8,4},{12,8},{0,12},{5,1},{9,5},{13,9},{1,13},{6,2},{10,6},{... | collective-permute-start | bytes 4423688 | tf_op jit(solution)/shard_map/ppermute | solution.py:21
  30.0 0.7 fusion.104
  44.1 0.7 fusion.102
  82.5 0.6 fusion.106
  83.2 8.6 %collective-permute-done.3 = f32[3,80,1536]{2,1,0:T(8,128)} collective-permute-done((f32[3,80,1536]{2,1,0:T(8,128)}, f32[3,80,1536]{2,1,0:T(8,128)}, u32[]{:S(2)}, u32[]{:S(2)}) %collective-permute-start.3) | collective-permute-done | bytes 1474592 | tf_op jit(solution)/shard_map/ppermute | solution.py:21
  91.8 1.6 pad_maximum_fusion
  94.0 0.4 fusion.15
  94.6 0.4 fusion.16
  95.2 0.4 fusion.14
  95.6 0.4 fusion.12
  96.0 0.4 fusion.13
  96.4 0.4 fusion.11
  98.1 3.0 %fusion.56 = f32[1,96,1536]{2,1,0:T(8,128)S(1)} fusion(f32[97,1537]{1,0:T(8,128)S(1)} %fusion.14, f32[97,1537]{1,0:T(8,128)S(1)} %fusion.15, f32[97,1537]{1,0:T(8,128)S(1)} %fusion.16, f32[]{:T(128)S(6)} %mul.523, f32[]{:T(128)S(6)} %mul.520, f32[]{:T(128)S(6)} %mul.517, f32[]{:T(128)S(6)} %mul.514, f32[]{:T(128)} %bitcast.31, f32[]{:T(128)S(6)} %mul.509, ...), kind=kLoop, calls=%fused_computation.130 | loop fusion | flops 3833856 | bytes 7667772 | tf_op jit(solution)/shard_map/stack | solution.py:136
  101.1 3.0 %fusion.41 = f32[1,96,1536]{2,1,0:T(8,128)S(1)} fusion(f32[97,1537]{1,0:T(8,128)S(1)} %fusion.11, f32[97,1537]{1,0:T(8,128)S(1)} %fusion.12, f32[97,1537]{1,0:T(8,128)S(1)} %fusion.13, f32[]{:T(128)S(6)} %mul.562, f32[]{:T(128)S(6)} %mul.559, f32[]{:T(128)S(6)} %mul.556, f32[]{:T(128)S(6)} %mul.553, f32[]{:T(128)S(6)} %mul.549, f32[]{:T(128)S(6)} %mul.546, ...), kind=kLoop, calls=%fused_computation.103 | loop fusion | flops 3833856 | bytes 7667772 | tf_op jit(solution)/shard_map/stack | solution.py:136
  104.1 3.0 %fusion.26 = f32[1,96,1536]{2,1,0:T(8,128)S(1)} fusion(f32[97,1537]{1,0:T(8,128)S(1)} %fusion.8, f32[97,1537]{1,0:T(8,128)S(1)} %fusion.9, f32[97,1537]{1,0:T(8,128)S(1)} %fusion.10, f32[]{:T(128)S(6)} %mul.601, f32[]{:T(128)S(6)} %mul.598, f32[]{:T(128)S(6)} %mul.595, f32[]{:T(128)S(6)} %mul.592, f32[]{:T(128)S(6)} %mul.588, f32[]{:T(128)S(6)} %mul.585, ...), kind=kLoop, calls=%fused_computation.76 | loop fusion | flops 3833856 | bytes 7667772 | tf_op jit(solution)/shard_map/stack | solution.py:136
  107.1 1.3 pad_maximum_fusion.3
  109.2 55.3 %all-reduce.2.cloned.1.call-done = f32[3,96,1536]{2,1,0:T(8,128)} async-done(((f32[3,96,1536]{2,1,0:T(8,128)}), f32[3,96,1536]{2,1,0:T(8,128)}) %all-reduce.2.cloned.1.call-update) | async-done | bytes 1769488 | tf_op jit(solution)/shard_map/psum | solution.py:138
  164.5 5.2 %cosine_multiply_fusion = (f32[3,96,768]{2,1,0:T(8,128)S(1)}, f32[3,96,768]{2,1,0:T(8,128)S(1)}) fusion(f32[3,96,1536]{2,1,0:T(8,128)} %all-reduce.2.cloned.1.call-done, s32[]{:T(128)S(6)} %select_n.305, f32[96,768]{1,0:T(8,128)} %param.20), kind=kLoop, calls=%fused_computation.44 | loop fusion | flops 442368 | bytes 2949124 | tf_op jit(solution)/shard_map/mul | solution.py:54
  170.3 3.1 %fusion.3 = f32[3,6,16,6,512]{4,2,3,1,0:T(8,128)S(1)} fusion(f32[3,6,16,6,128]{4,2,3,1,0:T(8,128)S(1)} %copy.19, f32[3,6,16,6,128]{4,2,3,1,0:T(8,128)S(1)} %copy.18, f32[128,256]{1,0:T(8,128)S(1)} %reshape.193, f32[128,256]{1,0:T(8,128)S(1)} %reshape.194, f32[128,256]{1,0:T(8,128)S(1)} %neg.18), kind=kOutput, calls=%fused_computation.14 | convolution fusion | flops 2718744576 | bytes 5701632 | tf_op jit(solution)/shard_map/sapnk,kj->sapnj/dot_general | solution.py:62
  173.4 5.8 %convolution_bitcast_fusion.1 = f32[3,6,32,6,512]{4,2,3,1,0:T(8,128)S(1)} fusion(f32[3,6,16,6,512]{4,2,3,1,0:T(8,128)S(1)} %fusion.3), kind=kOutput, calls=%fused_computation.9 | convolution fusion | flops 339745792 | bytes 10616832 | tf_op jit(solution)/shard_map/sapnj,up->saunj/dot_general | solution.py:64
  179.1 6.0 %convolution_bitcast_fusion.2 = f32[3,6,32,6,512]{4,2,3,1,0:T(8,128)S(1)} fusion(f32[3,6,16,6,512]{4,2,3,1,0:T(8,128)S(1)} %fusion.3), kind=kOutput, calls=%fused_computation.10 | convolution fusion | flops 339745792 | bytes 10616832 | tf_op jit(solution)/shard_map/sapnj,up->saunj/dot_general | solution.py:63
  185.2 3.4 %multiply_reduce_fusion.1 = (f32[3,6,6,256]{3,2,1,0:T(8,128)S(1)}, f32[3,6,6,256]{3,2,1,0:T(8,128)S(1)}, f32[3,6,6,256]{3,2,1,0:T(8,128)S(1)}) fusion(f32[32]{0:T(128)S(1)} %fusion.89, f32[256]{0:T(256)S(1)} %mul.613, f32[3,6,32,6,512]{4,2,3,1,0:T(8,128)S(1)} %convolution_bitcast_fusion.1, f32[3,6,32,6,512]{4,2,3,1,0:T(8,128)S(1)} %convolution_bitcast_fusion.2), kind=kLoop, calls=%fused_computation.7 | loop fusion | flops 8764416 | bytes 14488704 | tf_op jit(solution)/shard_map/reduce_sum | solution.py:75
  189.8 5.3 %fusion.7 = f32[2688]{0:T(1024)S(1)} fusion(bf16[3,2,6,48,2688]{4,3,2,1,0:T(8,128)(2,1)} %param.22, bf16[3,2,6,48,1]{3,2,0,1,4:T(8,128)(2,1)S(1)} %get-tuple-element.12), kind=kOutput, calls=%fused_computation.42 | convolution fusion | flops 9289728 | bytes 9303936 | tf_op jit(solution)/shard_map/dot_general | solution.py:141
  195.1 60.1 %psum.15 = f32[2688]{0:T(1024)S(1)} all-reduce(f32[2688]{0:T(1024)S(1)} %fusion.7), channel_id=1, replica_groups=mesh['runs'=2,'tile'=4,'layer'=2,'star'=2] {'tile','layer','star'}, use_global_device_ids=true, to_apply=%region_7.8 | all-reduce | flops 2688 | bytes 21504 | tf_op jit(solution)/shard_map/psum | solution.py:146
  255.2 0.6 copy.20
  255.8 0.6 multiply_subtract_fusion
  (58 shorter events, 6.1 us)
Async XLA Ops:
  7.2 157.3 %all-reduce.2.cloned.1.call-start = ((), (), s32[]{:S(2)}) async-start(), calls=%async_computation | async-start | bytes 3538944 | tf_op jit(solution)/shard_map/psum | solution.py:138
  8.2 12.5 %collective-permute-start = (f32[3,4,1536]{2,1,0:T(4,128)S(1)}, f32[3,4,1536]{2,1,0:T(4,128)S(1)}, u32[]{:S(2)}, u32[]{:S(2)}) collective-permute-start(f32[3,4,1536]{2,1,0:T(4,128)S(1)} %get-tuple-element.24), channel_id=1, source_target_pairs={{0,4},{4,8},{8,12},{12,0},{1,5},{5,9},{9,13},{13,1},{2,6},{6,10},{... | collective-permute-start | bytes 221192 | tf_op jit(solution)/shard_map/ppermute | solution.py:20
  11.3 9.4 %collective-permute-start.1 = (f32[3,4,1536]{2,1,0:T(4,128)S(1)}, f32[3,4,1536]{2,1,0:T(4,128)S(1)}, u32[]{:S(2)}, u32[]{:S(2)}) collective-permute-start(f32[3,4,1536]{2,1,0:T(4,128)S(1)} %get-tuple-element.25), channel_id=1, source_target_pairs={{4,0},{8,4},{12,8},{0,12},{5,1},{9,5},{13,9},{1,13},{6,2},{10,6},{... | collective-permute-start | bytes 221192 | tf_op jit(solution)/shard_map/ppermute | solution.py:21
  23.9 2.2 copy-start
  23.9 6.0 %copy-start.2 = (s32[6,6]{1,0:T(8,128)S(1)}, s32[6,6]{1,0:T(8,128)}, u32[]{:S(2)}) copy-start(s32[6,6]{1,0:T(8,128)} %param.16) | copy-start | bytes 436
  24.0 6.0 %copy-start.3 = (s32[6,6]{1,0:T(8,128)S(1)}, s32[6,6]{1,0:T(8,128)}, u32[]{:S(2)}) copy-start(s32[6,6]{1,0:T(8,128)} %param.17) | copy-start | bytes 436
  24.0 20.1 %copy-start.4 = (f32[6,6]{1,0:T(8,128)S(1)}, f32[6,6]{1,0:T(8,128)}, u32[]{:S(2)}) copy-start(f32[6,6]{1,0:T(8,128)} %param.19) | copy-start | bytes 436
  24.0 20.1 %copy-start.5 = (f32[6,6]{1,0:T(8,128)S(1)}, f32[6,6]{1,0:T(8,128)}, u32[]{:S(2)}) copy-start(f32[6,6]{1,0:T(8,128)} %param.18) | copy-start | bytes 436
  24.0 58.5 %copy-start.6 = (f32[3]{0:T(128)S(1)}, f32[3]{0:T(128)}, u32[]{:S(2)}) copy-start(f32[3]{0:T(128)} %param.13) | copy-start | bytes 40
  26.1 57.0 %collective-permute-start.2 = (f32[3,80,1536]{2,1,0:T(8,128)}, f32[3,80,1536]{2,1,0:T(8,128)S(1)}, u32[]{:S(2)}, u32[]{:S(2)}) collective-permute-start(f32[3,80,1536]{2,1,0:T(8,128)} %get-tuple-element.22), channel_id=1, source_target_pairs={{0,4},{4,8},{8,12},{12,0},{1,5},{5,9},{9,13},{13,1},{2,6},{6,10},{... | collective-permute-start | bytes 4423688 | tf_op jit(solution)/shard_map/ppermute | solution.py:20
  26.1 65.7 %collective-permute-start.3 = (f32[3,80,1536]{2,1,0:T(8,128)}, f32[3,80,1536]{2,1,0:T(8,128)}, u32[]{:S(2)}, u32[]{:S(2)}) collective-permute-start(f32[3,80,1536]{2,1,0:T(8,128)} %get-tuple-element.23), channel_id=1, source_target_pairs={{4,0},{8,4},{12,8},{0,12},{5,1},{9,5},{13,9},{1,13},{6,2},{10,6},{... | collective-permute-start | bytes 4423688 | tf_op jit(solution)/shard_map/ppermute | solution.py:21
  108.4 0.7 copy-start.7
  189.8 66.0 %copy-start.1 = (f32[2688]{0:T(1024)S(1)}, f32[2688]{0:T(1024)}, u32[]{:S(2)}) copy-start(f32[2688]{0:T(1024)} %param.23) | copy-start | bytes 32260
Sparse Core Ops, SparseCore 0:
  108.5 55.8 all-reduce.1
where the time goes:
time: 265 us; the launch traced here: 263 us
  between operations  71.4 us (27%)
  waiting for transfers between devices  63.9 us (24%)
  blocking collectives  60.1 us (23%)
  other arithmetic  28.6 us (11%)
  matrix products  20.2 us (8%)
  local copies, waits for them, and re-layouts  9.96 us (4%)
  starting transfers between devices  9.06 us (3%)
    psum x1, blocking collectives, body(): recon = lax.psum(local_terms, ('tile', 'layer', 'star'))  60.1 us
    psum x1, waiting for transfers between devices, body(): summed = lax.psum(partial_value, 'layer')  55.3 us
    another operation x4, other arithmetic, body(): partial_value = jnp.stack(pupils)  10.2 us
    ppermute x2, waiting for transfers between devices, with_halo(): after = lax.ppermute(first, axis, down)  8.64 us
    dot_general x1, matrix products, sh_slopes(): row_cos = jnp.einsum('sapnj,up->saunj', half, cosine, precision=highest)  6.05 us
    ppermute x2, starting transfers between devices, with_halo(): after = lax.ppermute(first, axis, down)  5.91 us
    dot_general x1, matrix products, sh_slopes(): row_sin = jnp.einsum('sapnj,up->saunj', half, sine, precision=highest)  5.76 us
  transfers between devices with their start and end apart: 5, of which 2 were waited for; matrix products, arithmetic and copies ran while one was open for 2% of the time, Pallas kernels for 0%

commit v1 on v0

--- a/solution.py
+++ b/solution.py
@@ -143,7 +143,7 @@
         recon_matrix.reshape(-1, recon_matrix.shape[-1]),
         preferred_element_type=jnp.float32,
     )[0]
-    recon = lax.psum(local_terms, ("tile", "layer", "star"))
+    recon = lax.psum(lax.psum(local_terms, "tile"), ("layer", "star"))
     commands = 2.0 * recon - prev_recon
     return (shifted, slopes, commands)
 

time: 265 us -> 233 us (0.88)
  blocking collectives: 60.1 us -> 28.9 us
    psum x1 -> x2, blocking collectives: 60.1 us -> 28.9 us  [body(): recon = lax.psum(lax.psum(local_terms, 'tile'), ('layer', 'star'))]
where the time goes in v1:
time: 233 us; the launch traced here: 232 us
  between operations  71.2 us (31%)
  waiting for transfers between devices  63.9 us (27%)
  blocking collectives  28.9 us (12%)
  other arithmetic  28.8 us (12%)
  matrix products  20.2 us (9%)
  local copies, waits for them, and re-layouts  10 us (4%)
  starting transfers between devices  9.06 us (4%)
    psum x1, waiting for transfers between devices, body(): summed = lax.psum(partial_value, 'layer')  55.3 us
    psum x2, blocking collectives, body(): recon = lax.psum(lax.psum(local_terms, 'tile'), ('layer', 'star'))  28.9 us
    another operation x4, other arithmetic, body(): partial_value = jnp.stack(pupils)  10.4 us
    ppermute x2, waiting for transfers between devices, with_halo(): after = lax.ppermute(first, axis, down)  8.55 us
    dot_general x1, matrix products, sh_slopes(): row_cos = jnp.einsum('sapnj,up->saunj', half, cosine, precision=highest)  6.05 us
    ppermute x2, starting transfers between devices, with_halo(): after = lax.ppermute(first, axis, down)  5.91 us
    dot_general x1, matrix products, sh_slopes(): row_sin = jnp.einsum('sapnj,up->saunj', half, sine, precision=highest)  5.76 us
    dot_general x1, matrix products, body(): jnp.dot(slopes.astype(jnp.bfloat16).reshape(1, -1), recon_matrix.reshape(...  5.29 us
  transfers between devices with their start and end apart: 5, of which 2 were waited for; matrix products, arithmetic and copies ran while one was open for 2% of the time, Pallas kernels for 0%

profile of v1, /device:TPU:0, one launch (start us, length us, event | category | flops | bytes accessed | tf_op | source)
XLA Modules:
  0.0 232.0 jit_solution(7134538177423129979)
XLA Ops:
  7.2 1.0 fusion.100
  8.2 3.1 %collective-permute-start = (f32[3,4,1536]{2,1,0:T(4,128)S(1)}, f32[3,4,1536]{2,1,0:T(4,128)S(1)}, u32[]{:S(2)}, u32[]{:S(2)}) collective-permute-start(f32[3,4,1536]{2,1,0:T(4,128)S(1)} %get-tuple-element.24), channel_id=1, source_target_pairs={{0,4},{4,8},{8,12},{12,0},{1,5},{5,9},{9,13},{13,1},{2,6},{6,10},{... | collective-permute-start | bytes 221192 | tf_op jit(solution)/shard_map/ppermute | solution.py:20
  11.3 2.1 collective-permute-start.1
  13.4 1.4 fusion.107
  20.5 1.7 pad_maximum_fusion.1
  23.7 2.1 fusion.99
  25.9 3.8 %collective-permute-start.3 = (f32[3,80,1536]{2,1,0:T(8,128)}, f32[3,80,1536]{2,1,0:T(8,128)}, u32[]{:S(2)}, u32[]{:S(2)}) collective-permute-start(f32[3,80,1536]{2,1,0:T(8,128)} %get-tuple-element.23), channel_id=1, source_target_pairs={{4,0},{8,4},{12,8},{0,12},{5,1},{9,5},{13,9},{1,13},{6,2},{10,6},{... | collective-permute-start | bytes 4423688 | tf_op jit(solution)/shard_map/ppermute | solution.py:21
  29.7 0.7 fusion.104
  43.8 0.8 fusion.102
  82.3 0.7 fusion.106
  83.0 8.5 %collective-permute-done.3 = f32[3,80,1536]{2,1,0:T(8,128)} collective-permute-done((f32[3,80,1536]{2,1,0:T(8,128)}, f32[3,80,1536]{2,1,0:T(8,128)}, u32[]{:S(2)}, u32[]{:S(2)}) %collective-permute-start.3) | collective-permute-done | bytes 1474592 | tf_op jit(solution)/shard_map/ppermute | solution.py:21
  91.5 1.6 pad_maximum_fusion
  93.7 0.4 fusion.15
  94.3 0.4 fusion.16
  94.9 0.4 fusion.14
  95.3 0.4 fusion.12
  95.8 0.4 fusion.13
  97.9 3.0 %fusion.56 = f32[1,96,1536]{2,1,0:T(8,128)S(1)} fusion(f32[97,1537]{1,0:T(8,128)S(1)} %fusion.14, f32[97,1537]{1,0:T(8,128)S(1)} %fusion.15, f32[97,1537]{1,0:T(8,128)S(1)} %fusion.16, f32[]{:T(128)S(6)} %mul.523, f32[]{:T(128)S(6)} %mul.520, f32[]{:T(128)S(6)} %mul.517, f32[]{:T(128)S(6)} %mul.514, f32[]{:T(128)} %bitcast.31, f32[]{:T(128)S(6)} %mul.509, ...), kind=kLoop, calls=%fused_computation.130 | loop fusion | flops 3833856 | bytes 7667772 | tf_op jit(solution)/shard_map/stack | solution.py:136
  100.9 3.0 %fusion.41 = f32[1,96,1536]{2,1,0:T(8,128)S(1)} fusion(f32[97,1537]{1,0:T(8,128)S(1)} %fusion.11, f32[97,1537]{1,0:T(8,128)S(1)} %fusion.12, f32[97,1537]{1,0:T(8,128)S(1)} %fusion.13, f32[]{:T(128)S(6)} %mul.562, f32[]{:T(128)S(6)} %mul.559, f32[]{:T(128)S(6)} %mul.556, f32[]{:T(128)S(6)} %mul.553, f32[]{:T(128)S(6)} %mul.549, f32[]{:T(128)S(6)} %mul.546, ...), kind=kLoop, calls=%fused_computation.103 | loop fusion | flops 3833856 | bytes 7667772 | tf_op jit(solution)/shard_map/stack | solution.py:136
  104.0 3.0 %fusion.26 = f32[1,96,1536]{2,1,0:T(8,128)S(1)} fusion(f32[97,1537]{1,0:T(8,128)S(1)} %fusion.8, f32[97,1537]{1,0:T(8,128)S(1)} %fusion.9, f32[97,1537]{1,0:T(8,128)S(1)} %fusion.10, f32[]{:T(128)S(6)} %mul.601, f32[]{:T(128)S(6)} %mul.598, f32[]{:T(128)S(6)} %mul.595, f32[]{:T(128)S(6)} %mul.592, f32[]{:T(128)S(6)} %mul.588, f32[]{:T(128)S(6)} %mul.585, ...), kind=kLoop, calls=%fused_computation.76 | loop fusion | flops 3833856 | bytes 7667772 | tf_op jit(solution)/shard_map/stack | solution.py:136
  107.0 1.3 pad_maximum_fusion.3
  109.1 55.3 %all-reduce.2.cloned.1.call-done = f32[3,96,1536]{2,1,0:T(8,128)} async-done(((f32[3,96,1536]{2,1,0:T(8,128)}), f32[3,96,1536]{2,1,0:T(8,128)}) %all-reduce.2.cloned.1.call-update) | async-done | bytes 1769488 | tf_op jit(solution)/shard_map/psum | solution.py:138
  164.4 5.2 %cosine_multiply_fusion = (f32[3,96,768]{2,1,0:T(8,128)S(1)}, f32[3,96,768]{2,1,0:T(8,128)S(1)}) fusion(f32[3,96,1536]{2,1,0:T(8,128)} %all-reduce.2.cloned.1.call-done, s32[]{:T(128)S(6)} %select_n.305, f32[96,768]{1,0:T(8,128)} %param.20), kind=kLoop, calls=%fused_computation.44 | loop fusion | flops 442368 | bytes 2949124 | tf_op jit(solution)/shard_map/mul | solution.py:54
  170.2 3.1 %fusion.3 = f32[3,6,16,6,512]{4,2,3,1,0:T(8,128)S(1)} fusion(f32[3,6,16,6,128]{4,2,3,1,0:T(8,128)S(1)} %copy.19, f32[3,6,16,6,128]{4,2,3,1,0:T(8,128)S(1)} %copy.18, f32[128,256]{1,0:T(8,128)S(1)} %reshape.193, f32[128,256]{1,0:T(8,128)S(1)} %reshape.194, f32[128,256]{1,0:T(8,128)S(1)} %neg.18), kind=kOutput, calls=%fused_computation.14 | convolution fusion | flops 2718744576 | bytes 5701632 | tf_op jit(solution)/shard_map/sapnk,kj->sapnj/dot_general | solution.py:62
  173.3 5.8 %convolution_bitcast_fusion.1 = f32[3,6,32,6,512]{4,2,3,1,0:T(8,128)S(1)} fusion(f32[3,6,16,6,512]{4,2,3,1,0:T(8,128)S(1)} %fusion.3), kind=kOutput, calls=%fused_computation.9 | convolution fusion | flops 339745792 | bytes 10616832 | tf_op jit(solution)/shard_map/sapnj,up->saunj/dot_general | solution.py:64
  179.0 6.0 %convolution_bitcast_fusion.2 = f32[3,6,32,6,512]{4,2,3,1,0:T(8,128)S(1)} fusion(f32[3,6,16,6,512]{4,2,3,1,0:T(8,128)S(1)} %fusion.3), kind=kOutput, calls=%fused_computation.10 | convolution fusion | flops 339745792 | bytes 10616832 | tf_op jit(solution)/shard_map/sapnj,up->saunj/dot_general | solution.py:63
  185.1 3.4 %multiply_reduce_fusion.1 = (f32[3,6,6,256]{3,2,1,0:T(8,128)S(1)}, f32[3,6,6,256]{3,2,1,0:T(8,128)S(1)}, f32[3,6,6,256]{3,2,1,0:T(8,128)S(1)}) fusion(f32[32]{0:T(128)S(1)} %fusion.89, f32[256]{0:T(256)S(1)} %mul.613, f32[3,6,32,6,512]{4,2,3,1,0:T(8,128)S(1)} %convolution_bitcast_fusion.1, f32[3,6,32,6,512]{4,2,3,1,0:T(8,128)S(1)} %convolution_bitcast_fusion.2), kind=kLoop, calls=%fused_computation.7 | loop fusion | flops 8764416 | bytes 14488704 | tf_op jit(solution)/shard_map/reduce_sum | solution.py:75
  189.7 5.3 %fusion.7 = f32[2688]{0:T(1024)S(1)} fusion(bf16[3,2,6,48,2688]{4,3,2,1,0:T(8,128)(2,1)} %param.22, bf16[3,2,6,48,1]{3,2,0,1,4:T(8,128)(2,1)S(1)} %get-tuple-element.12), kind=kOutput, calls=%fused_computation.42 | convolution fusion | flops 9289728 | bytes 9303936 | tf_op jit(solution)/shard_map/dot_general | solution.py:141
  195.0 18.7 %psum.22 = f32[2688]{0:T(1024)S(1)} all-reduce(f32[2688]{0:T(1024)S(1)} %fusion.7), channel_id=1, replica_groups=mesh['runs'=2,'tile'=4,'layer'=2,'star'=2] {'tile'}, use_global_device_ids=true, to_apply=%region_7.8 | all-reduce | flops 2688 | bytes 21504 | tf_op jit(solution)/shard_map/psum | solution.py:146
  213.7 10.2 %psum.23 = f32[2688]{0:T(1024)S(1)} all-reduce(f32[2688]{0:T(1024)S(1)} %psum.22), channel_id=1, replica_groups=mesh['runs'=2,'tile'=4,'layer'=2,'star'=2] {'layer','star'}, use_global_device_ids=true, to_apply=%region_8.9 | all-reduce | flops 2688 | bytes 21504 | tf_op jit(solution)/shard_map/psum | solution.py:146
  223.9 0.6 copy.20
  224.5 0.6 multiply_subtract_fusion
  (59 shorter events, 6.5 us)
Async XLA Ops:
  7.2 157.2 %all-reduce.2.cloned.1.call-start = ((), (), s32[]{:S(2)}) async-start(), calls=%async_computation | async-start | bytes 3538944 | tf_op jit(solution)/shard_map/psum | solution.py:138
  8.2 12.3 %collective-permute-start = (f32[3,4,1536]{2,1,0:T(4,128)S(1)}, f32[3,4,1536]{2,1,0:T(4,128)S(1)}, u32[]{:S(2)}, u32[]{:S(2)}) collective-permute-start(f32[3,4,1536]{2,1,0:T(4,128)S(1)} %get-tuple-element.24), channel_id=1, source_target_pairs={{0,4},{4,8},{8,12},{12,0},{1,5},{5,9},{9,13},{13,1},{2,6},{6,10},{... | collective-permute-start | bytes 221192 | tf_op jit(solution)/shard_map/ppermute | solution.py:20
  11.3 9.2 %collective-permute-start.1 = (f32[3,4,1536]{2,1,0:T(4,128)S(1)}, f32[3,4,1536]{2,1,0:T(4,128)S(1)}, u32[]{:S(2)}, u32[]{:S(2)}) collective-permute-start(f32[3,4,1536]{2,1,0:T(4,128)S(1)} %get-tuple-element.25), channel_id=1, source_target_pairs={{4,0},{8,4},{12,8},{0,12},{5,1},{9,5},{13,9},{1,13},{6,2},{10,6},{... | collective-permute-start | bytes 221192 | tf_op jit(solution)/shard_map/ppermute | solution.py:21
  23.7 2.2 copy-start
  23.7 6.0 %copy-start.2 = (s32[6,6]{1,0:T(8,128)S(1)}, s32[6,6]{1,0:T(8,128)}, u32[]{:S(2)}) copy-start(s32[6,6]{1,0:T(8,128)} %param.16) | copy-start | bytes 436
  23.7 6.0 %copy-start.3 = (s32[6,6]{1,0:T(8,128)S(1)}, s32[6,6]{1,0:T(8,128)}, u32[]{:S(2)}) copy-start(s32[6,6]{1,0:T(8,128)} %param.17) | copy-start | bytes 436
  23.7 20.1 %copy-start.4 = (f32[6,6]{1,0:T(8,128)S(1)}, f32[6,6]{1,0:T(8,128)}, u32[]{:S(2)}) copy-start(f32[6,6]{1,0:T(8,128)} %param.19) | copy-start | bytes 436
  23.7 20.1 %copy-start.5 = (f32[6,6]{1,0:T(8,128)S(1)}, f32[6,6]{1,0:T(8,128)}, u32[]{:S(2)}) copy-start(f32[6,6]{1,0:T(8,128)} %param.18) | copy-start | bytes 436
  23.7 58.6 %copy-start.6 = (f32[3]{0:T(128)S(1)}, f32[3]{0:T(128)}, u32[]{:S(2)}) copy-start(f32[3]{0:T(128)} %param.13) | copy-start | bytes 40
  25.9 57.1 %collective-permute-start.2 = (f32[3,80,1536]{2,1,0:T(8,128)}, f32[3,80,1536]{2,1,0:T(8,128)S(1)}, u32[]{:S(2)}, u32[]{:S(2)}) collective-permute-start(f32[3,80,1536]{2,1,0:T(8,128)} %get-tuple-element.22), channel_id=1, source_target_pairs={{0,4},{4,8},{8,12},{12,0},{1,5},{5,9},{9,13},{13,1},{2,6},{6,10},{... | collective-permute-start | bytes 4423688 | tf_op jit(solution)/shard_map/ppermute | solution.py:20
  25.9 65.7 %collective-permute-start.3 = (f32[3,80,1536]{2,1,0:T(8,128)}, f32[3,80,1536]{2,1,0:T(8,128)}, u32[]{:S(2)}, u32[]{:S(2)}) collective-permute-start(f32[3,80,1536]{2,1,0:T(8,128)} %get-tuple-element.23), channel_id=1, source_target_pairs={{4,0},{8,4},{12,8},{0,12},{5,1},{9,5},{13,9},{1,13},{6,2},{10,6},{... | collective-permute-start | bytes 4423688 | tf_op jit(solution)/shard_map/ppermute | solution.py:21
  108.3 0.7 copy-start.7
  189.7 34.8 %copy-start.1 = (f32[2688]{0:T(1024)S(1)}, f32[2688]{0:T(1024)}, u32[]{:S(2)}) copy-start(f32[2688]{0:T(1024)} %param.23) | copy-start | bytes 32260
Sparse Core Ops, SparseCore 0:
  108.4 55.8 all-reduce.1
